TPU v7x, 128 devices: a whole 4x4x4 slice. The times are simulated.
128 devices in a mesh: dp: 16 (over z, y_hi, core), tensor: 8 (over x, y_lo).
Axes of the slice: x: 4, y: 4 (y_hi: 2, y_lo: 2; y = y_hi * 2 + y_lo), z: 4, core: 2. Of those that a mesh axis runs over, the one named last changes fastest.
Arguments:
- train_states: bfloat16 [4096, 8192], P('dp'), may hold values from -6 to 6
- qkv_cotangent: bfloat16 [4096, 6144], P('dp', 'tensor'), may hold values from -0.09375 to 0.09375
- w_master: float32 [8192, 6144], P('dp', 'tensor'), may hold values from -1.1048543 to 1.1048543
- moment_one: float32 [8192, 6144], P('dp', 'tensor'), may hold values from -1.8 to 1.8
- moment_two: float32 [8192, 6144], P('dp', 'tensor'), may hold values from 0.02 to 2
- prompt_states: bfloat16 [8192, 8192], P('dp'), may hold values from -45 to 45
- norm_gain: float32 [8192], replicated, may hold values from 0.1 to 1.9
- w_out: bfloat16 [4096, 8192], P('tensor'), may hold values from -0.09375 to 0.09375
Outputs:
- update_dir: float32 [8192, 6144], P('dp', 'tensor')
- prefill_out: bfloat16 [8192, 8192], P(('dp', 'tensor'))
All inputs are finite; a program needn't handle non-finite values.
Results may differ from a plain program's by a relative error of at most 0.02.
Values may be sent and summed in bfloat16 or wider, within the bound.
A program may use at most 128 MiB of HBM per device.

v0:
```python
import jax
import jax.numpy as jnp
from jax import lax
from jax.sharding import PartitionSpec as P

HD = 128
beta_one = 0.9
beta_two = 0.95
bias_one = 1.0 - 0.9**8
bias_two = 1.0 - 0.95**8
learn_rate = 0.002
adam_eps = 1e-08
norm_eps = 1e-05
rope_base = 500000.0


def rope_tables(length, head_size):
    half_width = head_size // 2
    exponent = jnp.arange(half_width, dtype=jnp.float32) * (2.0 / head_size)
    inverse = jnp.power(jnp.float32(rope_base), -exponent)
    position = jnp.arange(length, dtype=jnp.float32)
    angles = position[:, None] * inverse[None, :]
    cosine_table = jnp.concatenate([jnp.cos(angles), jnp.cos(angles)], axis=1)
    sine_table = jnp.concatenate([jnp.sin(angles), jnp.sin(angles)], axis=1)
    return (cosine_table, sine_table)


def rotate(head_block, cosine_table, sine_table):
    half_width = head_block.shape[-1] // 2
    turned = jnp.concatenate([-head_block[..., half_width:], head_block[..., :half_width]], axis=-1)
    return head_block * cosine_table + turned * sine_table


def body(
    train_states, qkv_cotangent, w_master, moment_one, moment_two, prompt_states, norm_gain, w_out
):
    slice_width = w_master.shape[1]
    gradient = lax.psum_scatter(
        lax.dot_general(
            train_states,
            qkv_cotangent,
            (((0,), (0,)), ((), ())),
            preferred_element_type=jnp.float32,
        ).astype(jnp.bfloat16),
        "dp",
        scatter_dimension=0,
        tiled=True,
    ).astype(jnp.float32)
    moment_new = beta_one * moment_one + (1.0 - beta_one) * gradient
    second_new = beta_two * moment_two + (1.0 - beta_two) * gradient * gradient
    update_dir = moment_new / bias_one / (jnp.sqrt(second_new / bias_two) + adam_eps)
    owned_weight = (w_master - learn_rate * update_dir).astype(jnp.bfloat16)
    length = prompt_states.shape[0]
    widened = prompt_states.astype(jnp.float32)
    mean_square = jnp.mean(widened * widened, axis=1, keepdims=True)
    normed = (widened * lax.rsqrt(mean_square + norm_eps) * norm_gain).astype(jnp.bfloat16)
    projected = jnp.dot(
        normed,
        lax.all_gather(owned_weight, "dp", axis=0, tiled=True),
        preferred_element_type=jnp.float32,
    )
    query_width = slice_width - 2 * HD
    head_count = query_width // HD
    score_scale = HD ** (-0.5)
    cosine_table, sine_table = rope_tables(length, HD)
    queries = projected[:, :query_width].reshape(length, head_count, HD)
    queries = (
        rotate(queries, cosine_table[:, None, :], sine_table[:, None, :]) * score_scale
    ).astype(jnp.bfloat16)
    key_rows = rotate(
        projected[:, query_width : query_width + HD], cosine_table, sine_table
    ).astype(jnp.bfloat16)
    value_rows = projected[:, query_width + HD :].astype(jnp.bfloat16)
    scores = jnp.einsum("qhd,kd->hqk", queries, key_rows, preferred_element_type=jnp.float32)
    causal = jnp.arange(length)[:, None] >= jnp.arange(length)[None, :]
    scores = jnp.where(causal[None], scores, -jnp.inf)
    attend_weights = jax.nn.softmax(scores, axis=-1).astype(jnp.bfloat16)
    attended = jnp.einsum(
        "hqk,kd->qhd", attend_weights, value_rows, preferred_element_type=jnp.float32
    ).astype(jnp.bfloat16)
    attended = attended.reshape(length, query_width)
    summed = lax.psum_scatter(
        jnp.dot(attended, w_out, preferred_element_type=jnp.float32).astype(jnp.bfloat16),
        "tensor",
        scatter_dimension=0,
        tiled=True,
    )
    return (update_dir, summed)


def solution(mesh):
    placed = (
        P("dp", None),
        P("dp", "tensor"),
        P("dp", "tensor"),
        P("dp", "tensor"),
        P("dp", "tensor"),
        P("dp", None),
        P(),
        P("tensor", None),
    )
    return jax.shard_map(
        body,
        mesh=mesh,
        in_specs=placed,
        out_specs=(P("dp", "tensor"), P(("dp", "tensor"), None)),
        check_vma=False,
    )
```

profile of v0, /device:TPU:1, one launch (start us, length us, event | category | flops | bytes accessed | tf_op | source)
XLA Modules:
  0.0 435.9 jit_solution(55790417744570518)
XLA Ops:
  7.2 0.0 copy-start
  7.2 0.0 reduce-scatter.3.cloned.1.call-start
  7.2 0.9 copy-done
  8.2 10.2 %convolution_convert_fusion = bf16[8192,768]{1,0:T(8,128)(2,1)} fusion(bf16[256,8192]{1,0:T(8,128)(2,1)} %param.8, bf16[256,768]{1,0:T(8,128)(2,1)S(1)} %copy-done), kind=kOutput, calls=%fused_computation.6 | convolution fusion | flops 3227516928 | bytes 17170432 | tf_op jit(solution)/shard_map/dot_general | solution.py:39
  18.4 0.0 copy-start.2
  18.4 0.0 copy-start.3
  18.4 0.0 reduce-scatter.3.cloned.1.call-update
  18.4 0.0 all-gather.2.cloned.1.call-start
  18.5 125.2 %reduce-scatter.3.cloned.1.call-done = bf16[512,768]{1,0:T(8,128)(2,1)} async-done(((bf16[8192,768]{1,0:T(8,128)(2,1)}), bf16[512,768]{1,0:T(8,128)(2,1)}) %reduce-scatter.3.cloned.1.call-update) | async-done | bytes 786448 | tf_op jit(solution)/shard_map/reduce_scatter | solution.py:38
  143.7 0.0 copy-done.2
  143.7 0.0 copy-done.3
  143.7 4.2 subtract_convert_fusion
  147.9 0.0 all-gather.2.cloned.1.call-update
  147.9 0.2 reduce-scatter.5.cloned.1.call-start
  148.2 0.1 iota_compare_fusion
  148.3 1.0 fusion.31
  149.3 0.2 pad_maximum_fusion
  149.5 0.0 copy-start.4
  149.5 5.1 %fusion.1 = f32[512]{0:T(512)S(1)} fusion(bf16[512,8192]{1,0:T(8,128)(2,1)} %param.13), kind=kLoop, calls=%fused_computation.3 | loop fusion | flops 12582400 | bytes 8390656 | tf_op jit(solution)/shard_map/reduce_sum | solution.py:55
  154.6 83.7 %all-gather.2.cloned.1.call-done = bf16[8192,768]{1,0:T(8,128)(2,1)} async-done(((bf16[512,768]{1,0:T(8,128)(2,1)}), bf16[8192,768]{1,0:T(8,128)(2,1)}) %all-gather.2.cloned.1.call-update) | async-done | bytes 12582928 | tf_op jit(solution)/shard_map/all_gather | solution.py:59
  238.3 0.0 copy-done.4
  238.3 12.0 %fusion.4 = f32[512,768]{1,0:T(8,128)S(1)} fusion(bf16[8192,768]{1,0:T(8,128)(2,1)} %all-gather.2.cloned.1.call-done, bf16[512,8192]{1,0:T(8,128)(2,1)} %param.13, f32[8192]{0:T(1024)S(1)} %copy-done.4, f32[512]{0:T(512)S(1)} %add_rsqrt_fusion), kind=kOutput, calls=%fused_computation.8 | convolution fusion | flops 6459228160 | bytes 22579200 | tf_op jit(solution)/shard_map/dot_general | solution.py:57
  250.3 0.1 copy_bitcast_fusion
  250.4 0.1 slice_negate_fusion.1
  250.5 0.3 slice_negate_fusion
  250.9 0.9 fusion.23
  251.8 0.0 slice-start
  251.8 1.9 fusion.40
  253.7 0.0 slice-start.1
  253.7 0.5 fusion.19
  254.2 0.0 slice-done
  254.2 1.8 slice-done.1
  256.0 6.9 %convolution_convert_fusion.1 = bf16[512,8192]{1,0:T(8,128)(2,1)} fusion(bf16[512,512]{0,1:T(8,128)(2,1)S(1)} %bitcast.37, bf16[512,8192]{1,0:T(8,128)(2,1)S(1)} %bitcast.36), kind=kOutput, calls=%fused_computation.7 | convolution fusion | flops 4299161600 | bytes 17301504 | tf_op jit(solution)/shard_map/dot_general | solution.py:83
  262.8 0.0 copy-start.1
  262.8 0.0 reduce-scatter.5.cloned.1.call-update
  262.9 166.5 %reduce-scatter.5.cloned.1.call-done = bf16[64,8192]{1,0:T(8,128)(2,1)} async-done(((bf16[512,8192]{1,0:T(8,128)(2,1)}), bf16[64,8192]{1,0:T(8,128)(2,1)}) %reduce-scatter.5.cloned.1.call-update) | async-done | bytes 1048592 | tf_op jit(solution)/shard_map/reduce_scatter | solution.py:82
  429.4 0.0 copy-done.1
  (3 shorter events, 0.0 us)
Async XLA Ops:
  7.2 1.0 copy-start
  7.2 136.5 %reduce-scatter.3.cloned.1.call-start = ((), (), s32[]{:S(2)}) async-start(), calls=%async_computation.2 | async-start | bytes 13369344 | tf_op jit(solution)/shard_map/reduce_scatter | solution.py:38
  18.4 125.3 %copy-start.2 = (f32[512,768]{1,0:T(8,128)S(1)}, f32[512,768]{1,0:T(8,128)}, u32[]{:S(2)}) copy-start(f32[512,768]{1,0:T(8,128)} %param.10) | copy-start | bytes 4718596
  18.4 125.3 %copy-start.3 = (f32[512,768]{1,0:T(8,128)S(1)}, f32[512,768]{1,0:T(8,128)}, u32[]{:S(2)}) copy-start(f32[512,768]{1,0:T(8,128)} %param.12) | copy-start | bytes 4718596
  18.4 219.8 %all-gather.2.cloned.1.call-start = ((), (), s32[]{:S(2)}) async-start(), calls=%async_computation.3 | async-start | bytes 13369344 | tf_op jit(solution)/shard_map/all_gather | solution.py:59
  147.9 281.5 %reduce-scatter.5.cloned.1.call-start = ((), (), s32[]{:S(2)}) async-start(), calls=%async_computation.4 | async-start | bytes 9437184 | tf_op jit(solution)/shard_map/reduce_scatter | solution.py:82
  149.5 88.8 %copy-start.4 = (f32[8192]{0:T(1024)S(1)}, f32[8192]{0:T(1024)}, u32[]{:S(2)}) copy-start(f32[8192]{0:T(1024)} %param.14) | copy-start | bytes 98308
  251.8 2.4 slice-start
  253.7 2.3 slice-start.1
  262.8 166.6 %copy-start.1 = (bf16[256,768]{1,0:T(8,128)(2,1)S(1)}, bf16[256,768]{1,0:T(8,128)(2,1)}, u32[]{:S(2)}) copy-start(bf16[256,768]{1,0:T(8,128)(2,1)} %param.9) | copy-start | bytes 1179652
Sparse Core Ops, SparseCore 0:
  18.6 125.0 reduce-scatter.2
  148.1 90.1 all-gather.1
  263.0 166.3 reduce-scatter.4
where the time goes:
time: 436 us
  waiting for transfers between devices  375 us (86%)
  matrix products  30.5 us (7%)
  between operations  13.9 us (3%)
  other arithmetic  13 us (3%)
    reduce_scatter x1, waiting for transfers between devices, body(): lax.psum_scatter(jnp.dot(attended, w_out, preferred_element_type=jnp.floa...  167 us
    reduce_scatter x1, waiting for transfers between devices, body(): lax.psum_scatter(lax.dot_general(train_states, qkv_cotangent, (((0,), (0,...  125 us
    all_gather x1, waiting for transfers between devices, body(): lax.all_gather(owned_weight, 'dp', axis=0, tiled=True)  83.7 us
    dot_general x1, matrix products, body(): jnp.dot(normed, lax.all_gather(owned_weight, 'dp', axis=0, tiled=True), p...  12 us
    dot_general x1, matrix products, body(): lax.dot_general(train_states, qkv_cotangent, (((0,), (0,)), ((), ())), pr...  10.2 us
  transfers between devices with their start and end apart: 3, of which 3 were waited for; matrix products, arithmetic and copies ran while one was open for 1% of the time, Pallas kernels for 0%

commit v1 on v0

--- a/solution.py
+++ b/solution.py
@@ -56,7 +56,9 @@
     normed = (widened * lax.rsqrt(mean_square + norm_eps) * norm_gain).astype(jnp.bfloat16)
     projected = jnp.dot(
         normed,
-        lax.all_gather(owned_weight, "dp", axis=0, tiled=True),
+        jnp.concatenate(
+            lax.all_to_all(jnp.stack([owned_weight] * lax.axis_size("dp")), "dp", 0, 0), axis=0
+        ),
         preferred_element_type=jnp.float32,
     )
     query_width = slice_width - 2 * HD

time: 436 us -> 500 us (1.15)
  waiting for transfers between devices: 375 us -> 427 us
  starting transfers between devices: 0.3 us -> 6.21 us
  local copies, waits for them, and re-layouts: 2.8 us -> 8.51 us
    all_to_all x0 -> x1, waiting for transfers between devices: none -> 134 us  [body(): lax.all_to_all(jnp.stack([owned_weight] * lax.axis_size('dp')), 'dp', 0, 0)]
    all_gather x1 -> x0, waiting for transfers between devices: 83.7 us -> none  [body(): lax.all_gather(owned_weight, 'dp', axis=0, tiled=True)]
    all_to_all x0 -> x1, starting transfers between devices: none -> 5.95 us  [body(): lax.all_to_all(jnp.stack([owned_weight] * lax.axis_size('dp')), 'dp', 0, 0)]
    another operation x0 -> x1, local copies, waits for them, and re-layouts: none -> 5.71 us  [body(): jnp.stack([owned_weight] * lax.axis_size('dp'))]
where the time goes in v1:
time: 500 us; the launch traced here: 499 us
  waiting for transfers between devices  427 us (85%)
  matrix products  30.7 us (6%)
  between operations  14.2 us (3%)
  other arithmetic  13.2 us (3%)
  local copies, waits for them, and re-layouts  8.51 us (2%)
  starting transfers between devices  6.21 us (1%)
    reduce_scatter x1, waiting for transfers between devices, body(): lax.psum_scatter(jnp.dot(attended, w_out, preferred_element_type=jnp.floa...  167 us
    all_to_all x1, waiting for transfers between devices, body(): lax.all_to_all(jnp.stack([owned_weight] * lax.axis_size('dp')), 'dp', 0, 0)  134 us
    reduce_scatter x1, waiting for transfers between devices, body(): lax.psum_scatter(lax.dot_general(train_states, qkv_cotangent, (((0,), (0,...  125 us
    dot_general x1, matrix products, body(): jnp.dot(normed, jnp.concatenate(lax.all_to_all(jnp.stack([owned_weight] *...  12 us
    dot_general x1, matrix products, body(): lax.dot_general(train_states, qkv_cotangent, (((0,), (0,)), ((), ())), pr...  10.2 us
  transfers between devices with their start and end apart: 3, of which 3 were waited for; matrix products, arithmetic and copies ran while one was open for 1% of the time, Pallas kernels for 0%

profile of v1, /device:TPU:1, one launch (start us, length us, event | category | flops | bytes accessed | tf_op | source)
XLA Modules:
  0.0 499.5 jit_solution(2786637096994930954)
XLA Ops:
  7.2 0.0 copy-start
  7.2 0.0 reduce-scatter.3.cloned.1.call-start
  7.2 0.9 copy-done
  8.2 10.2 %convolution_convert_fusion = bf16[8192,768]{1,0:T(8,128)(2,1)} fusion(bf16[256,8192]{1,0:T(8,128)(2,1)} %param.8, bf16[256,768]{1,0:T(8,128)(2,1)S(1)} %copy-done), kind=kOutput, calls=%fused_computation.6 | convolution fusion | flops 3227516928 | bytes 17170432 | tf_op jit(solution)/shard_map/dot_general | solution.py:39
  18.4 0.0 copy-start.2
  18.4 0.0 reduce-scatter.3.cloned.1.call-update
  18.4 125.2 %reduce-scatter.3.cloned.1.call-done = bf16[512,768]{1,0:T(8,128)(2,1)} async-done(((bf16[8192,768]{1,0:T(8,128)(2,1)}), bf16[512,768]{1,0:T(8,128)(2,1)}) %reduce-scatter.3.cloned.1.call-update) | async-done | bytes 786448 | tf_op jit(solution)/shard_map/reduce_scatter | solution.py:38
  143.7 0.0 copy-done.2
  143.7 4.5 subtract_convert_fusion
  148.1 5.7 %stack.2 = bf16[16,512,768]{2,1,0:T(8,128)(2,1)} broadcast(bf16[512,768]{1,0:T(8,128)(2,1)S(1)} %get-tuple-element.2), dimensions={1,2} | broadcast | bytes 13369344 | tf_op jit(solution)/shard_map/stack | solution.py:60
  153.8 6.0 %all-to-all-start = ((bf16[16,512,768]{2,1,0:T(8,128)(2,1)}), bf16[16,512,768]{2,1,0:T(8,128)(2,1)}, u32[]{:S(2)}, u32[]{:S(2)}) async-start(bf16[16,512,768]{2,1,0:T(8,128)(2,1)} %stack.2), calls=%async_computation.1 | async-start | bytes 25165824 | tf_op jit(solution)/shard_map/all_to_all | solution.py:60
  159.8 0.2 reduce-scatter.5.cloned.1.call-start
  160.0 0.1 iota_compare_fusion
  160.1 1.0 fusion.31
  161.1 0.2 pad_maximum_fusion
  161.3 0.0 copy-start.3
  161.3 5.1 %fusion.1 = f32[512]{0:T(512)S(1)} fusion(bf16[512,8192]{1,0:T(8,128)(2,1)} %param.13), kind=kLoop, calls=%fused_computation.3 | loop fusion | flops 12582400 | bytes 8390656 | tf_op jit(solution)/shard_map/reduce_sum | solution.py:55
  166.4 134.4 %all-to-all-done = bf16[16,512,768]{2,1,0:T(8,128)(2,1)} async-done(((bf16[16,512,768]{2,1,0:T(8,128)(2,1)}), bf16[16,512,768]{2,1,0:T(8,128)(2,1)}, u32[]{:S(2)}, u32[]{:S(2)}) %all-to-all-start) | async-done | bytes 12582944 | tf_op jit(solution)/shard_map/all_to_all | solution.py:60
  300.9 0.0 copy-done.3
  300.9 12.0 %fusion.4 = f32[512,768]{1,0:T(8,128)S(1)} fusion(bf16[8192,768]{1,0:T(8,128)(2,1)} %bitcast, bf16[512,8192]{1,0:T(8,128)(2,1)} %param.13, f32[8192]{0:T(1024)S(1)} %copy-done.3, f32[512]{0:T(512)S(1)} %add_rsqrt_fusion), kind=kOutput, calls=%fused_computation.8 | convolution fusion | flops 6459228160 | bytes 22579200 | tf_op jit(solution)/shard_map/dot_general | solution.py:57
  312.9 0.1 copy_bitcast_fusion
  313.0 0.1 slice_negate_fusion.1
  313.1 0.3 slice_negate_fusion
  313.5 0.9 fusion.23
  314.4 0.0 slice-start
  314.4 1.9 fusion.40
  316.3 0.0 slice-start.1
  316.3 0.5 fusion.19
  316.8 0.0 slice-done
  316.8 1.8 slice-done.1
  318.6 7.0 %convolution_convert_fusion.1 = bf16[512,8192]{1,0:T(8,128)(2,1)} fusion(bf16[512,512]{0,1:T(8,128)(2,1)S(1)} %bitcast.38, bf16[512,8192]{1,0:T(8,128)(2,1)S(1)} %bitcast.37), kind=kOutput, calls=%fused_computation.7 | convolution fusion | flops 4299161600 | bytes 17301504 | tf_op jit(solution)/shard_map/dot_general | solution.py:85
  325.6 0.0 copy-start.1
  325.6 0.0 reduce-scatter.5.cloned.1.call-update
  325.6 167.0 %reduce-scatter.5.cloned.1.call-done = bf16[64,8192]{1,0:T(8,128)(2,1)} async-done(((bf16[512,8192]{1,0:T(8,128)(2,1)}), bf16[64,8192]{1,0:T(8,128)(2,1)}) %reduce-scatter.5.cloned.1.call-update) | async-done | bytes 1048592 | tf_op jit(solution)/shard_map/reduce_scatter | solution.py:84
  492.6 0.0 copy-done.1
  (3 shorter events, 0.0 us)
Async XLA Ops:
  7.2 1.0 copy-start
  7.2 136.5 %reduce-scatter.3.cloned.1.call-start = ((), (), s32[]{:S(2)}) async-start(), calls=%async_computation.3 | async-start | bytes 13369344 | tf_op jit(solution)/shard_map/reduce_scatter | solution.py:38
  18.4 125.3 %copy-start.2 = (f32[512,768]{1,0:T(8,128)S(1)}, f32[512,768]{1,0:T(8,128)}, u32[]{:S(2)}) copy-start(f32[512,768]{1,0:T(8,128)} %param.10) | copy-start | bytes 4718596
  153.8 147.0 %all-to-all-start = ((bf16[16,512,768]{2,1,0:T(8,128)(2,1)}), bf16[16,512,768]{2,1,0:T(8,128)(2,1)}, u32[]{:S(2)}, u32[]{:S(2)}) async-start(bf16[16,512,768]{2,1,0:T(8,128)(2,1)} %stack.2), calls=%async_computation.1 | async-start | bytes 25165824 | tf_op jit(solution)/shard_map/all_to_all | solution.py:60
  159.8 332.8 %reduce-scatter.5.cloned.1.call-start = ((), (), s32[]{:S(2)}) async-start(), calls=%async_computation.4 | async-start | bytes 9437184 | tf_op jit(solution)/shard_map/reduce_scatter | solution.py:84
  161.3 139.5 %copy-start.3 = (f32[8192]{0:T(1024)S(1)}, f32[8192]{0:T(1024)}, u32[]{:S(2)}) copy-start(f32[8192]{0:T(1024)} %param.14) | copy-start | bytes 98308
  314.4 2.4 slice-start
  316.3 2.3 slice-start.1
  325.6 167.1 %copy-start.1 = (bf16[256,768]{1,0:T(8,128)(2,1)S(1)}, bf16[256,768]{1,0:T(8,128)(2,1)}, u32[]{:S(2)}) copy-start(bf16[256,768]{1,0:T(8,128)(2,1)} %param.9) | copy-start | bytes 1179652
Sparse Core Ops, SparseCore 0:
  18.6 125.0 reduce-scatter.2
  325.7 166.8 reduce-scatter.4
